TPU v7x, 512 devices: a whole 4x4x16 slice. The times are simulated.
512 devices in a mesh: space: 64 (over x, z), node: 4 (over y_hi, core), tm: 2 (over y_lo).
Axes of the slice: x: 4, y: 4 (y_hi: 2, y_lo: 2; y = y_hi * 2 + y_lo), z: 16, core: 2. Of those that a mesh axis runs over, the one named last changes fastest.
Arguments:
- start_old: float32 [2, 512, 128, 256], P('tm', 'space'), may hold values from -4 to 4
- nodes_old: float32 [2, 4, 512, 128, 256], P('tm', 'node', 'space'), may hold values from -4 to 4
Outputs:
- nodes_new: float32 [2, 4, 512, 128, 256], P('tm', 'node', 'space')
- end_new: float32 [2, 512, 128, 256], P('tm', 'space')
All inputs are finite; a program needn't handle non-finite values.
Results may differ from a plain program's by a relative error of at most 0.00002.
Values sent between devices are 32-bit elements; how exact they have to be, the bound alone decides.
A program may use at most 64 MiB of HBM per device.

v0:
```python
import jax
import jax.numpy as jnp
from jax import lax
from jax.sharding import PartitionSpec as P

NODES = 4
PASSES = 4
time_step = 0.25
diffusion = 4.0
reaction = 1.0


def padded_2(block, sides, width):
    for axis, dim in sides:
        count = lax.axis_size(axis)
        forward = [(i, i + 1) for i in range(count - 1)]
        forward.append((count - 1, 0))
        backward = [(target, source) for source, target in forward]
        low = lax.ppermute(
            lax.slice_in_dim(block, block.shape[dim] - width, None, axis=dim), axis, forward
        )
        high = lax.ppermute(lax.slice_in_dim(block, 0, width, axis=dim), axis, backward)
        block = jnp.concatenate([low, block, high], axis=dim)
    return block


def shifted_2(array, axis, by):
    size = lax.axis_size(axis)
    pairs = [(i, i + by) for i in range(size) if 0 <= i + by < size]
    return lax.ppermute(array, axis, pairs)


def collocation(count):
    points = [-0.8611363115940526, -0.3399810435848563, 0.3399810435848563, 0.8611363115940526]
    raw_weights = [0.3478548451374538, 0.6521451548625461, 0.6521451548625461, 0.3478548451374538]
    node_times = [(point + 1.0) / 2.0 for point in points]
    quadrature = [[0.0 for column in range(count)] for target in range(count)]
    for source in range(count):
        coeffs = [1.0]
        scaling = 1.0
        for other in range(count):
            if other != source:
                other_time = node_times[other]
                shifted = [0.0] + coeffs
                for power in range(len(coeffs)):
                    shifted[power] = shifted[power] - other_time * coeffs[power]
                coeffs = shifted
                scaling = scaling * (node_times[source] - other_time)
        for target in range(count):
            target_time = node_times[target]
            integral = 0.0
            for power in range(len(coeffs)):
                integral = integral + coeffs[power] * target_time ** (power + 1) / (power + 1)
            quadrature[target][source] = integral / scaling
    return (node_times, quadrature, [weight / 2.0 for weight in raw_weights])


def neighbour_sum(padded):
    inner = padded[1:-1]
    total = padded[2:] + padded[:-2]
    total = total + jnp.roll(inner, -1, 1) + jnp.roll(inner, 1, 1)
    total = total + jnp.roll(inner, -1, 2) + jnp.roll(inner, 1, 2)
    return total


def forcing(values, padded):
    laplace = neighbour_sum(padded) - 6.0 * values
    return (laplace, diffusion * laplace + reaction * (values - values * values * values))


def on_device(start_old, nodes_old):
    node_times, quadrature, weights = collocation(NODES)
    node_index = lax.axis_index("node")
    node_time = jnp.asarray(node_times, jnp.float32)[node_index]
    weight_table = jnp.asarray(weights, jnp.float32)
    node_weight = weight_table[node_index]
    quad_table = jnp.asarray(quadrature, jnp.float32)
    state_old = nodes_old[0, 0]
    start_state = start_old[0]
    padded = padded_2(state_old, (("space", 0),), 1)
    laplace_old, force_old = forcing(state_old, padded)
    quad_row = quad_table[node_index]
    shard_piece = lax.all_gather(force_old[None], "node", axis=0, tiled=True)
    quad_part = jnp.sum(quad_row[:, None, None, None] * shard_piece, axis=0)
    weight_part = jnp.sum(weight_table[:, None, None, None] * shard_piece, axis=0)
    end_old = start_state + time_step * weight_part
    received = shifted_2(end_old, "tm", 1)
    begin_state = jnp.where(lax.axis_index("tm") == 0, start_state, received)
    implicit = time_step * diffusion * node_time
    right_side = begin_state + time_step * quad_part - implicit * laplace_old
    divisor = 1.0 + 6.0 * implicit
    iterate = state_old
    for step_index in range(PASSES):
        widened = padded_2(iterate, (("space", 0),), 1)
        iterate = (right_side + implicit * neighbour_sum(widened)) / divisor
    padded_new = padded_2(iterate, (("space", 0),), 1)
    laplace_new, force_new = forcing(iterate, padded_new)
    weighted_new = lax.psum(node_weight * force_new, "node")
    end_new = begin_state + time_step * weighted_new
    return (iterate[None, None], end_new[None])


def solution(mesh):
    return jax.shard_map(
        on_device,
        mesh=mesh,
        in_specs=(P("tm", "space", None, None), P("tm", "node", "space", None, None)),
        out_specs=(P("tm", "node", "space", None, None), P("tm", "space", None, None)),
        check_vma=False,
    )
```

profile of v0, /device:TPU:1, one launch (start us, length us, event | category | flops | bytes accessed | tf_op | source)
XLA Modules:
  0.0 228.6 jit_solution(15902153033855880192)
XLA Ops:
  7.2 0.0 copy-start
  7.2 0.0 all-gather.3.cloned.1.call-start
  7.2 1.1 slice_bitcast_fusion.1
  8.3 14.1 %collective-permute-start = (f32[1,128,256]{2,1,0:T(8,128)S(1)}, f32[1,128,256]{2,1,0:T(8,128)S(1)}, u32[]{:S(2)}, u32[]{:S(2)}) collective-permute-start(f32[1,128,256]{2,1,0:T(8,128)S(1)} %get-tuple-element.48), channel_id=1, source_target_pairs={{8,0},{16,8},{24,16},{32,24},{40,32},{48,40},{56,48},{64,56},{72,6... | collective-permute-start | bytes 393224 | tf_op jit(solution)/shard_map/ppermute | solution.py:22
  22.4 1.9 collective-permute-start.1
  24.4 1.4 fusion.63
  25.8 1.9 fusion.62
  27.7 0.0 copy-done
  27.7 0.2 fusion.60
  27.9 0.0 collective-permute-done
  27.9 3.5 %collective-permute-done.1 = f32[1,128,256]{2,1,0:T(8,128)S(1)} collective-permute-done((f32[1,128,256]{2,1,0:T(8,128)S(1)}, f32[1,128,256]{2,1,0:T(8,128)S(1)}, u32[]{:S(2)}, u32[]{:S(2)}) %collective-permute-start.1) | collective-permute-done | bytes 131104 | tf_op jit(solution)/shard_map/ppermute | solution.py:19
  31.5 0.0 copy-start.3
  31.5 2.2 fusion
  33.7 0.0 all-gather.3.cloned.1.call-update
  33.7 0.0 all-reduce.2.cloned.1.call-start
  33.8 0.8 dynamic-slice_bitcast_fusion
  34.5 38.3 %all-gather.3.cloned.1.call-done = f32[32,128,256]{2,1,0:T(8,128)} async-done(((f32[8,128,256]{2,1,0:T(8,128)}), f32[32,128,256]{2,1,0:T(8,128)}) %all-gather.3.cloned.1.call-update) | async-done | bytes 4194320 | tf_op jit(solution)/shard_map/all_gather | solution.py:83
  72.8 0.0 copy-done.3
  72.8 4.1 %multiply_reduce_fusion.1 = (f32[8,128,256]{2,1,0:T(8,128)S(1)}, f32[8,128,256]{2,1,0:T(8,128)}) fusion(f32[4,8,128,256]{3,2,1,0:T(8,128)} %bitcast.30, f32[4]{0:T(128)S(1)} %copy-done.3, f32[4]{0:T(128)S(1)} %dynamic-slice_bitcast_fusion), kind=kLoop, calls=%fused_computation.1 | loop fusion | flops 3670016 | bytes 6291488 | tf_op jit(solution)/shard_map/reduce_sum | solution.py:85
  76.9 0.0 copy-done.2
  76.9 1.1 bitcast_add_fusion
  78.0 2.3 collective-permute-start.2
  80.3 0.7 dynamic_slice.11
  81.0 0.0 copy-done.4
  81.0 0.6 dynamic_slice.10
  82.1 20.7 %collective-permute-done.2 = f32[8,128,256]{2,1,0:T(8,128)S(1)} collective-permute-done((f32[8,128,256]{2,1,0:T(8,128)}, f32[8,128,256]{2,1,0:T(8,128)S(1)}, u32[]{:S(2)}, u32[]{:S(2)}) %collective-permute-start.2) | collective-permute-done | bytes 1048608 | tf_op jit(solution)/shard_map/ppermute | solution.py:30
  102.8 2.5 %add_divide_fusion = (f32[8,128,256]{2,1,0:T(8,128)S(1)}, f32[8,128,256]{2,1,0:T(8,128)S(1)}) fusion(f32[8,128,256]{2,1,0:T(8,128)} %get-tuple-element.7, f32[]{:T(128)S(6)} %add.127, f32[]{:T(128)} %bitcast.6, f32[1,1,8,128,256]{4,3,2,1,0:T(8,128)S(1)} %copy-done, f32[8,128,256]{2,1,0:T(8,128)} %get-tuple-element.3, ...), kind=kLoop, calls=%fused_computation.56 | loop fusion | flops 2621440 | bytes 7340041 | tf_op jit(solution)/shard_map/div | solution.py:95
  105.3 0.2 fusion.55
  105.5 0.2 fusion.58
  105.7 0.4 fusion.56
  106.0 7.8 %collective-permute-start.3 = (f32[1,128,256]{2,1,0:T(8,128)S(1)}, f32[1,128,256]{2,1,0:T(8,128)S(1)}, u32[]{:S(2)}, u32[]{:S(2)}) collective-permute-start(f32[1,128,256]{2,1,0:T(8,128)S(1)} %get-tuple-element.46), channel_id=1, source_target_pairs={{8,0},{16,8},{24,16},{32,24},{40,32},{48,40},{56,48},{64,56},{72,6... | collective-permute-start | bytes 393224 | tf_op jit(solution)/shard_map/ppermute | solution.py:22
  113.9 1.9 collective-permute-start.4
  115.8 0.0 collective-permute-done.3
  115.8 7.1 %collective-permute-done.4 = f32[1,128,256]{2,1,0:T(8,128)S(1)} collective-permute-done((f32[1,128,256]{2,1,0:T(8,128)S(1)}, f32[1,128,256]{2,1,0:T(8,128)S(1)}, u32[]{:S(2)}, u32[]{:S(2)}) %collective-permute-start.4) | collective-permute-done | bytes 131104 | tf_op jit(solution)/shard_map/ppermute | solution.py:19
  122.9 1.2 fusion.33
  124.1 0.2 fusion.50
  124.3 0.2 fusion.53
  124.5 0.4 fusion.51
  124.9 1.9 collective-permute-start.5
  126.8 3.4 %collective-permute-start.6 = (f32[1,128,256]{2,1,0:T(8,128)S(1)}, f32[1,128,256]{2,1,0:T(8,128)S(1)}, u32[]{:S(2)}, u32[]{:S(2)}) collective-permute-start(f32[1,128,256]{2,1,0:T(8,128)S(1)} %get-tuple-element.37), channel_id=1, source_target_pairs={{0,8},{8,16},{16,24},{24,32},{32,40},{40,48},{48,56},{56,64},{64,7... | collective-permute-start | bytes 393224 | tf_op jit(solution)/shard_map/ppermute | solution.py:19
  130.2 0.4 collective-permute-done.5
  130.6 5.2 %collective-permute-done.6 = f32[1,128,256]{2,1,0:T(8,128)S(1)} collective-permute-done((f32[1,128,256]{2,1,0:T(8,128)S(1)}, f32[1,128,256]{2,1,0:T(8,128)S(1)}, u32[]{:S(2)}, u32[]{:S(2)}) %collective-permute-start.6) | collective-permute-done | bytes 131104 | tf_op jit(solution)/shard_map/ppermute | solution.py:19
  135.9 1.2 fusion.25
  137.1 0.2 fusion.45
  137.3 0.2 fusion.48
  137.5 0.4 fusion.46
  137.9 1.9 collective-permute-start.7
  139.8 3.4 %collective-permute-start.8 = (f32[1,128,256]{2,1,0:T(8,128)S(1)}, f32[1,128,256]{2,1,0:T(8,128)S(1)}, u32[]{:S(2)}, u32[]{:S(2)}) collective-permute-start(f32[1,128,256]{2,1,0:T(8,128)S(1)} %get-tuple-element.27), channel_id=1, source_target_pairs={{0,8},{8,16},{16,24},{24,32},{32,40},{40,48},{48,56},{56,64},{64,7... | collective-permute-start | bytes 393224 | tf_op jit(solution)/shard_map/ppermute | solution.py:19
  143.2 0.4 collective-permute-done.7
  143.6 5.2 %collective-permute-done.8 = f32[1,128,256]{2,1,0:T(8,128)S(1)} collective-permute-done((f32[1,128,256]{2,1,0:T(8,128)S(1)}, f32[1,128,256]{2,1,0:T(8,128)S(1)}, u32[]{:S(2)}, u32[]{:S(2)}) %collective-permute-start.8) | collective-permute-done | bytes 131104 | tf_op jit(solution)/shard_map/ppermute | solution.py:19
  148.8 1.2 fusion.17
  150.1 0.0 copy-start.1
  150.1 0.2 fusion.40
  150.3 0.2 fusion.43
  150.5 0.4 fusion.41
  150.9 1.9 collective-permute-start.9
  152.8 3.4 %collective-permute-start.10 = (f32[1,128,256]{2,1,0:T(8,128)S(1)}, f32[1,128,256]{2,1,0:T(8,128)S(1)}, u32[]{:S(2)}, u32[]{:S(2)}) collective-permute-start(f32[1,128,256]{2,1,0:T(8,128)S(1)} %get-tuple-element.17), channel_id=1, source_target_pairs={{0,8},{8,16},{16,24},{24,32},{32,40},{40,48},{48,56},{56,64},{64,7... | collective-permute-start | bytes 393224 | tf_op jit(solution)/shard_map/ppermute | solution.py:19
  156.2 0.4 collective-permute-done.9
  156.6 5.2 %collective-permute-done.10 = f32[1,128,256]{2,1,0:T(8,128)S(1)} collective-permute-done((f32[1,128,256]{2,1,0:T(8,128)S(1)}, f32[1,128,256]{2,1,0:T(8,128)S(1)}, u32[]{:S(2)}, u32[]{:S(2)}) %collective-permute-start.10) | collective-permute-done | bytes 131104 | tf_op jit(solution)/shard_map/ppermute | solution.py:19
  161.8 0.0 copy-done.1
  161.8 2.4 %fusion.2 = f32[8,128,256]{2,1,0:T(8,128)} fusion(f32[8,128,256]{2,1,0:T(8,128)S(1)} %fusion.17, f32[1,128,256]{2,1,0:T(8,128)S(1)} %collective-permute-done.10, f32[1,128,256]{2,1,0:T(8,128)S(1)} %collective-permute-done.9, f32[8,1,256]{2,1,0:T(1,128)S(1)} %get-tuple-element.13, f32[8,127,256]{2,1,0:T(8,128)S(1)} %get-tuple-element.15, ...), kind=kLoop, calls=%fused_computation.6 | loop fusion | flops 4980736 | bytes 6553604 | tf_op jit(solution)/shard_map/mul | solution.py:98
  164.2 0.0 all-reduce.2.cloned.1.call-update
  164.3 55.1 %all-reduce.2.cloned.1.call-done = f32[8,128,256]{2,1,0:T(8,128)} async-done(((f32[8,128,256]{2,1,0:T(8,128)}), f32[8,128,256]{2,1,0:T(8,128)}) %all-reduce.2.cloned.1.call-update) | async-done | bytes 1048592 | tf_op jit(solution)/shard_map/psum | solution.py:98
  219.4 2.4 %add_bitcast_fusion = f32[1,8,128,256]{3,2,1,0:T(8,128)} fusion(f32[8,128,256]{2,1,0:T(8,128)} %all-reduce.2.cloned.1.call-done, f32[8,128,256]{2,1,0:T(8,128)S(1)} %collective-permute-done.2, f32[1,8,128,256]{3,2,1,0:T(8,128)S(1)} %copy-done.2, pred[]{:T(512)S(6)} %eq.3), kind=kLoop, calls=%fused_computation.55 | loop fusion | flops 786432 | bytes 4194305 | tf_op jit(solution)/shard_map/broadcast_in_dim | solution.py:100
  (11 shorter events, 0.2 us)
Async XLA Ops:
  7.2 20.5 %copy-start = (f32[1,1,8,128,256]{4,3,2,1,0:T(8,128)S(1)}, f32[1,1,8,128,256]{4,3,2,1,0:T(8,128)}, u32[]{:S(2)}) copy-start(f32[1,1,8,128,256]{4,3,2,1,0:T(8,128)} %param.6) | copy-start | bytes 3145732
  7.2 65.7 %all-gather.3.cloned.1.call-start = ((), (), s32[]{:S(2)}) async-start(), calls=%async_computation.1 | async-start | bytes 5242880 | tf_op jit(solution)/shard_map/all_gather | solution.py:83
  8.3 19.6 %collective-permute-start = (f32[1,128,256]{2,1,0:T(8,128)S(1)}, f32[1,128,256]{2,1,0:T(8,128)S(1)}, u32[]{:S(2)}, u32[]{:S(2)}) collective-permute-start(f32[1,128,256]{2,1,0:T(8,128)S(1)} %get-tuple-element.48), channel_id=1, source_target_pairs={{8,0},{16,8},{24,16},{32,24},{40,32},{48,40},{56,48},{64,56},{72,6... | collective-permute-start | bytes 393224 | tf_op jit(solution)/shard_map/ppermute | solution.py:22
  22.4 9.0 %collective-permute-start.1 = (f32[1,128,256]{2,1,0:T(8,128)S(1)}, f32[1,128,256]{2,1,0:T(8,128)S(1)}, u32[]{:S(2)}, u32[]{:S(2)}) collective-permute-start(f32[1,128,256]{2,1,0:T(8,128)S(1)} %get-tuple-element.49), channel_id=1, source_target_pairs={{0,8},{8,16},{16,24},{24,32},{32,40},{40,48},{48,56},{56,64},{64,7... | collective-permute-start | bytes 393224 | tf_op jit(solution)/shard_map/ppermute | solution.py:19
  31.5 41.4 %copy-start.3 = (f32[4]{0:T(128)S(1)}, f32[4]{0:T(128)}, u32[]{:S(2)}) copy-start(f32[4]{0:T(128)} %constant.30.clone) | copy-start | bytes 52
  33.7 43.2 %copy-start.2 = (f32[1,8,128,256]{3,2,1,0:T(8,128)S(1)}, f32[1,8,128,256]{3,2,1,0:T(8,128)}, u32[]{:S(2)}) copy-start(f32[1,8,128,256]{3,2,1,0:T(8,128)} %param.5) | copy-start | bytes 3145732
  33.7 185.7 %all-reduce.2.cloned.1.call-start = ((), (), s32[]{:S(2)}) async-start(), calls=%async_computation | async-start | bytes 2097152 | tf_op jit(solution)/shard_map/psum | solution.py:98
  72.8 8.1 %copy-start.4 = (f32[4]{0:T(128)S(1)}, f32[4]{0:T(128)}, u32[]{:S(2)}) copy-start(f32[4]{0:T(128)} %constant.29.clone) | copy-start | bytes 52
  78.0 24.7 %collective-permute-start.2 = (f32[8,128,256]{2,1,0:T(8,128)}, f32[8,128,256]{2,1,0:T(8,128)S(1)}, u32[]{:S(2)}, u32[]{:S(2)}) collective-permute-start(f32[8,128,256]{2,1,0:T(8,128)} %bitcast_add_fusion), channel_id=1, source_target_pairs={{0,1},{2,3},{4,5},{6,7},{8,9},{10,11},{12,13},{14,15},{16,17},{18,... | collective-permute-start | bytes 3145736 | tf_op jit(solution)/shard_map/ppermute | solution.py:30
  106.0 9.8 %collective-permute-start.3 = (f32[1,128,256]{2,1,0:T(8,128)S(1)}, f32[1,128,256]{2,1,0:T(8,128)S(1)}, u32[]{:S(2)}, u32[]{:S(2)}) collective-permute-start(f32[1,128,256]{2,1,0:T(8,128)S(1)} %get-tuple-element.46), channel_id=1, source_target_pairs={{8,0},{16,8},{24,16},{32,24},{40,32},{48,40},{56,48},{64,56},{72,6... | collective-permute-start | bytes 393224 | tf_op jit(solution)/shard_map/ppermute | solution.py:22
  113.9 9.0 %collective-permute-start.4 = (f32[1,128,256]{2,1,0:T(8,128)S(1)}, f32[1,128,256]{2,1,0:T(8,128)S(1)}, u32[]{:S(2)}, u32[]{:S(2)}) collective-permute-start(f32[1,128,256]{2,1,0:T(8,128)S(1)} %get-tuple-element.47), channel_id=1, source_target_pairs={{0,8},{8,16},{16,24},{24,32},{32,40},{40,48},{48,56},{56,64},{64,7... | collective-permute-start | bytes 393224 | tf_op jit(solution)/shard_map/ppermute | solution.py:19
  124.9 5.7 %collective-permute-start.5 = (f32[1,128,256]{2,1,0:T(8,128)S(1)}, f32[1,128,256]{2,1,0:T(8,128)S(1)}, u32[]{:S(2)}, u32[]{:S(2)}) collective-permute-start(f32[1,128,256]{2,1,0:T(8,128)S(1)} %get-tuple-element.36), channel_id=1, source_target_pairs={{8,0},{16,8},{24,16},{32,24},{40,32},{48,40},{56,48},{64,56},{72,6... | collective-permute-start | bytes 393224 | tf_op jit(solution)/shard_map/ppermute | solution.py:22
  126.8 9.0 %collective-permute-start.6 = (f32[1,128,256]{2,1,0:T(8,128)S(1)}, f32[1,128,256]{2,1,0:T(8,128)S(1)}, u32[]{:S(2)}, u32[]{:S(2)}) collective-permute-start(f32[1,128,256]{2,1,0:T(8,128)S(1)} %get-tuple-element.37), channel_id=1, source_target_pairs={{0,8},{8,16},{16,24},{24,32},{32,40},{40,48},{48,56},{56,64},{64,7... | collective-permute-start | bytes 393224 | tf_op jit(solution)/shard_map/ppermute | solution.py:19
  137.9 5.7 %collective-permute-start.7 = (f32[1,128,256]{2,1,0:T(8,128)S(1)}, f32[1,128,256]{2,1,0:T(8,128)S(1)}, u32[]{:S(2)}, u32[]{:S(2)}) collective-permute-start(f32[1,128,256]{2,1,0:T(8,128)S(1)} %get-tuple-element.26), channel_id=1, source_target_pairs={{8,0},{16,8},{24,16},{32,24},{40,32},{48,40},{56,48},{64,56},{72,6... | collective-permute-start | bytes 393224 | tf_op jit(solution)/shard_map/ppermute | solution.py:22
  139.8 9.0 %collective-permute-start.8 = (f32[1,128,256]{2,1,0:T(8,128)S(1)}, f32[1,128,256]{2,1,0:T(8,128)S(1)}, u32[]{:S(2)}, u32[]{:S(2)}) collective-permute-start(f32[1,128,256]{2,1,0:T(8,128)S(1)} %get-tuple-element.27), channel_id=1, source_target_pairs={{0,8},{8,16},{16,24},{24,32},{32,40},{40,48},{48,56},{56,64},{64,7... | collective-permute-start | bytes 393224 | tf_op jit(solution)/shard_map/ppermute | solution.py:19
  150.1 11.8 %copy-start.1 = (f32[8,128,256]{2,1,0:T(8,128)}, f32[8,128,256]{2,1,0:T(8,128)S(1)}, u32[]{:S(2)}) copy-start(f32[8,128,256]{2,1,0:T(8,128)S(1)} %fusion.17) | copy-start | bytes 3145732
  150.9 5.7 %collective-permute-start.9 = (f32[1,128,256]{2,1,0:T(8,128)S(1)}, f32[1,128,256]{2,1,0:T(8,128)S(1)}, u32[]{:S(2)}, u32[]{:S(2)}) collective-permute-start(f32[1,128,256]{2,1,0:T(8,128)S(1)} %get-tuple-element.16), channel_id=1, source_target_pairs={{8,0},{16,8},{24,16},{32,24},{40,32},{48,40},{56,48},{64,56},{72,6... | collective-permute-start | bytes 393224 | tf_op jit(solution)/shard_map/ppermute | solution.py:22
  152.8 9.0 %collective-permute-start.10 = (f32[1,128,256]{2,1,0:T(8,128)S(1)}, f32[1,128,256]{2,1,0:T(8,128)S(1)}, u32[]{:S(2)}, u32[]{:S(2)}) collective-permute-start(f32[1,128,256]{2,1,0:T(8,128)S(1)} %get-tuple-element.17), channel_id=1, source_target_pairs={{0,8},{8,16},{16,24},{24,32},{32,40},{40,48},{48,56},{56,64},{64,7... | collective-permute-start | bytes 393224 | tf_op jit(solution)/shard_map/ppermute | solution.py:19
Sparse Core Ops, SparseCore 0:
  33.8 38.9 all-gather.2
  164.4 54.9 all-reduce.1
where the time goes:
time: 229 us
  waiting for transfers between devices  142 us (62%)
  starting transfers between devices  44 us (19%)
  other arithmetic  18.3 us (8%)
  between operations  14.9 us (7%)
  local copies, waits for them, and re-layouts  9.72 us (4%)
    psum x1, waiting for transfers between devices, on_device(): weighted_new = lax.psum(node_weight * force_new, 'node')  55.1 us
    all_gather x1, waiting for transfers between devices, on_device(): shard_piece = lax.all_gather(force_old[None], 'node', axis=0, tiled=True)  38.3 us
    ppermute x5, starting transfers between devices, padded_2(): lax.ppermute(lax.slice_in_dim(block, 0, width, axis=dim), axis, backward)  27.7 us
    ppermute x5, waiting for transfers between devices, padded_2(): lax.ppermute(lax.slice_in_dim(block, block.shape[dim] - width, None, axis...  26.4 us
    ppermute x1, waiting for transfers between devices, shifted_2(): return lax.ppermute(array, axis, pairs)  20.7 us
    ppermute x5, starting transfers between devices, padded_2(): lax.ppermute(lax.slice_in_dim(block, block.shape[dim] - width, None, axis...  13.9 us
    div x4, other arithmetic, on_device(): iterate = (right_side + implicit * neighbour_sum(widened)) / divisor  6.12 us
    slice x10, local copies, waits for them, and re-layouts, neighbour_sum(): total = total + jnp.roll(inner, -1, 2) + jnp.roll(inner, 1, 2)  5.54 us
  transfers between devices with their start and end apart: 13, of which 11 were waited for; matrix products, arithmetic and copies ran while one was open for 2% of the time, Pallas kernels for 0%

commit v1 on v0

--- a/solution.py
+++ b/solution.py
@@ -80,7 +80,9 @@
     padded = padded_2(state_old, (("space", 0),), 1)
     laplace_old, force_old = forcing(state_old, padded)
     quad_row = quad_table[node_index]
-    shard_piece = lax.all_gather(force_old[None], "node", axis=0, tiled=True)
+    shard_piece = jnp.concatenate(
+        lax.all_to_all(jnp.stack([force_old[None]] * lax.axis_size("node")), "node", 0, 0), axis=0
+    )
     quad_part = jnp.sum(quad_row[:, None, None, None] * shard_piece, axis=0)
     weight_part = jnp.sum(weight_table[:, None, None, None] * shard_piece, axis=0)
     end_old = start_state + time_step * weight_part

time: 229 us -> 244 us (1.066)
  waiting for transfers between devices: 142 us -> 150 us
  starting transfers between devices: 44 us -> 47.5 us
  local copies, waits for them, and re-layouts: 9.72 us -> 12.3 us
    all_to_all x0 -> x1, waiting for transfers between devices: none -> 48 us  [on_device(): lax.all_to_all(jnp.stack([force_old[None]] * lax.axis_size('node')), 'nod...]
    all_gather x1 -> x0, waiting for transfers between devices: 38.3 us -> none  [on_device(): shard_piece = lax.all_gather(force_old[None], 'node', axis=0, tiled=True)]
    all_to_all x0 -> x1, starting transfers between devices: none -> 7.04 us  [on_device(): lax.all_to_all(jnp.stack([force_old[None]] * lax.axis_size('node')), 'nod...]
    ppermute x5, starting transfers between devices: 27.7 us -> 22.2 us  [padded_2(): lax.ppermute(lax.slice_in_dim(block, 0, width, axis=dim), axis, backward)]
    another operation x0 -> x1, local copies, waits for them, and re-layouts: none -> 2.51 us  [on_device(): jnp.stack([force_old[None]] * lax.axis_size('node'))]
  transfers between devices with their start and end apart: 13 -> 13, of which waited for: 11 -> 12; matrix products, arithmetic and copies ran while one was open for 2% -> 2% of each run, Pallas kernels for 0% -> 0%
where the time goes in v1:
time: 244 us; the launch traced here: 243 us
  waiting for transfers between devices  150 us (61%)
  starting transfers between devices  47.5 us (19%)
  other arithmetic  18.5 us (8%)
  between operations  15 us (6%)
  local copies, waits for them, and re-layouts  12.3 us (5%)
    psum x1, waiting for transfers between devices, on_device(): weighted_new = lax.psum(node_weight * force_new, 'node')  55.2 us
    all_to_all x1, waiting for transfers between devices, on_device(): lax.all_to_all(jnp.stack([force_old[None]] * lax.axis_size('node')), 'nod...  48 us
    ppermute x5, waiting for transfers between devices, padded_2(): lax.ppermute(lax.slice_in_dim(block, block.shape[dim] - width, None, axis...  24.9 us
    ppermute x5, starting transfers between devices, padded_2(): lax.ppermute(lax.slice_in_dim(block, 0, width, axis=dim), axis, backward)  22.2 us
    ppermute x1, waiting for transfers between devices, shifted_2(): return lax.ppermute(array, axis, pairs)  19.8 us
    ppermute x5, starting transfers between devices, padded_2(): lax.ppermute(lax.slice_in_dim(block, block.shape[dim] - width, None, axis...  15 us
    all_to_all x1, starting transfers between devices, on_device(): lax.all_to_all(jnp.stack([force_old[None]] * lax.axis_size('node')), 'nod...  7.04 us
    div x4, other arithmetic, on_device(): iterate = (right_side + implicit * neighbour_sum(widened)) / divisor  6.62 us
  transfers between devices with their start and end apart: 13, of which 12 were waited for; matrix products, arithmetic and copies ran while one was open for 2% of the time, Pallas kernels for 0%

profile of v1, /device:TPU:1, one launch (start us, length us, event | category | flops | bytes accessed | tf_op | source)
XLA Modules:
  0.0 242.8 jit_solution(6196258791063640015)
XLA Ops:
  7.2 0.0 copy-start
  7.2 1.1 slice_bitcast_fusion.1
  8.3 14.1 %collective-permute-start = (f32[1,128,256]{2,1,0:T(8,128)S(1)}, f32[1,128,256]{2,1,0:T(8,128)S(1)}, u32[]{:S(2)}, u32[]{:S(2)}) collective-permute-start(f32[1,128,256]{2,1,0:T(8,128)S(1)} %get-tuple-element.48), channel_id=1, source_target_pairs={{8,0},{16,8},{24,16},{32,24},{40,32},{48,40},{56,48},{64,56},{72,6... | collective-permute-start | bytes 393224 | tf_op jit(solution)/shard_map/ppermute | solution.py:22
  22.4 1.9 collective-permute-start.1
  24.3 1.4 fusion.65
  25.7 1.9 fusion.64
  27.6 0.0 copy-done
  27.6 0.2 fusion.62
  27.9 0.0 collective-permute-done
  27.9 3.5 %collective-permute-done.1 = f32[1,128,256]{2,1,0:T(8,128)S(1)} collective-permute-done((f32[1,128,256]{2,1,0:T(8,128)S(1)}, f32[1,128,256]{2,1,0:T(8,128)S(1)}, u32[]{:S(2)}, u32[]{:S(2)}) %collective-permute-start.1) | collective-permute-done | bytes 131104 | tf_op jit(solution)/shard_map/ppermute | solution.py:19
  31.4 1.9 fusion.2
  33.3 2.5 %stack.3 = f32[4,1,8,128,256]{4,3,2,1,0:T(8,128)} broadcast(f32[8,128,256]{2,1,0:T(8,128)S(1)} %get-tuple-element.6), dimensions={2,3,4} | broadcast | bytes 5242880 | tf_op jit(solution)/shard_map/stack | solution.py:84
  35.8 0.0 copy-start.3
  35.8 7.0 %all-to-all-start = ((f32[4,1,8,128,256]{4,3,2,1,0:T(8,128)}), f32[4,1,8,128,256]{4,3,2,1,0:T(8,128)}, u32[]{:S(2)}, u32[]{:S(2)}) async-start(f32[4,1,8,128,256]{4,3,2,1,0:T(8,128)} %stack.3), calls=%async_computation | async-start | bytes 8388608 | tf_op jit(solution)/shard_map/all_to_all | solution.py:84
  42.8 0.0 all-reduce.2.cloned.1.call-start
  42.8 0.8 dynamic-slice_bitcast_fusion
  43.6 48.0 %all-to-all-done = f32[4,1,8,128,256]{4,3,2,1,0:T(8,128)} async-done(((f32[4,1,8,128,256]{4,3,2,1,0:T(8,128)}), f32[4,1,8,128,256]{4,3,2,1,0:T(8,128)}, u32[]{:S(2)}, u32[]{:S(2)}) %all-to-all-start) | async-done | bytes 4194336 | tf_op jit(solution)/shard_map/all_to_all | solution.py:84
  91.6 0.0 copy-done.3
  91.6 4.1 %fusion = (f32[8,128,256]{2,1,0:T(8,128)S(1)}, f32[8,128,256]{2,1,0:T(8,128)}) fusion(f32[4,1,8,128,256]{4,3,2,1,0:T(8,128)} %all-to-all-done, f32[4]{0:T(128)S(1)} %copy-done.3, f32[4]{0:T(128)S(1)} %dynamic-slice_bitcast_fusion), kind=kLoop, calls=%fused_computation.2 | loop fusion | flops 3670016 | bytes 6291488 | tf_op jit(solution)/shard_map/reduce_sum | solution.py:87
  95.7 0.0 copy-done.2
  95.7 1.1 bitcast_add_fusion
  96.8 3.3 %collective-permute-start.2 = (f32[8,128,256]{2,1,0:T(8,128)}, f32[8,128,256]{2,1,0:T(8,128)S(1)}, u32[]{:S(2)}, u32[]{:S(2)}) collective-permute-start(f32[8,128,256]{2,1,0:T(8,128)} %bitcast_add_fusion), channel_id=1, source_target_pairs={{0,1},{2,3},{4,5},{6,7},{8,9},{10,11},{12,13},{14,15},{16,17},{18,... | collective-permute-start | bytes 3145736 | tf_op jit(solution)/shard_map/ppermute | solution.py:30
  100.1 0.7 dynamic_slice.11
  100.7 0.0 copy-done.4
  100.7 0.6 dynamic_slice.10
  102.1 19.8 %collective-permute-done.2 = f32[8,128,256]{2,1,0:T(8,128)S(1)} collective-permute-done((f32[8,128,256]{2,1,0:T(8,128)}, f32[8,128,256]{2,1,0:T(8,128)S(1)}, u32[]{:S(2)}, u32[]{:S(2)}) %collective-permute-start.2) | collective-permute-done | bytes 1048608 | tf_op jit(solution)/shard_map/ppermute | solution.py:30
  121.8 2.6 %add_divide_fusion = (f32[8,128,256]{2,1,0:T(8,128)S(1)}, f32[8,128,256]{2,1,0:T(8,128)S(1)}) fusion(f32[8,128,256]{2,1,0:T(8,128)} %get-tuple-element.7, f32[]{:T(128)S(6)} %add.127, f32[]{:T(128)} %bitcast.6, f32[1,1,8,128,256]{4,3,2,1,0:T(8,128)S(1)} %copy-done, f32[8,128,256]{2,1,0:T(8,128)} %get-tuple-element.3, ...), kind=kLoop, calls=%fused_computation.58 | loop fusion | flops 2621440 | bytes 7340041 | tf_op jit(solution)/shard_map/div | solution.py:97
  124.5 0.2 fusion.57
  124.7 0.2 fusion.60
  124.9 0.4 fusion.58
  125.2 2.3 collective-permute-start.3
  127.5 3.0 %collective-permute-start.4 = (f32[1,128,256]{2,1,0:T(8,128)S(1)}, f32[1,128,256]{2,1,0:T(8,128)S(1)}, u32[]{:S(2)}, u32[]{:S(2)}) collective-permute-start(f32[1,128,256]{2,1,0:T(8,128)S(1)} %get-tuple-element.47), channel_id=1, source_target_pairs={{0,8},{8,16},{16,24},{24,32},{32,40},{40,48},{48,56},{56,64},{64,7... | collective-permute-start | bytes 393224 | tf_op jit(solution)/shard_map/ppermute | solution.py:19
  130.5 0.4 collective-permute-done.3
  130.9 5.6 %collective-permute-done.4 = f32[1,128,256]{2,1,0:T(8,128)S(1)} collective-permute-done((f32[1,128,256]{2,1,0:T(8,128)S(1)}, f32[1,128,256]{2,1,0:T(8,128)S(1)}, u32[]{:S(2)}, u32[]{:S(2)}) %collective-permute-start.4) | collective-permute-done | bytes 131104 | tf_op jit(solution)/shard_map/ppermute | solution.py:19
  136.5 1.3 fusion.35
  137.9 0.2 fusion.52
  138.1 0.2 fusion.55
  138.3 0.4 fusion.53
  138.7 1.9 collective-permute-start.5
  140.6 3.4 %collective-permute-start.6 = (f32[1,128,256]{2,1,0:T(8,128)S(1)}, f32[1,128,256]{2,1,0:T(8,128)S(1)}, u32[]{:S(2)}, u32[]{:S(2)}) collective-permute-start(f32[1,128,256]{2,1,0:T(8,128)S(1)} %get-tuple-element.37), channel_id=1, source_target_pairs={{0,8},{8,16},{16,24},{24,32},{32,40},{40,48},{48,56},{56,64},{64,7... | collective-permute-start | bytes 393224 | tf_op jit(solution)/shard_map/ppermute | solution.py:19
  144.0 0.4 collective-permute-done.5
  144.4 5.2 %collective-permute-done.6 = f32[1,128,256]{2,1,0:T(8,128)S(1)} collective-permute-done((f32[1,128,256]{2,1,0:T(8,128)S(1)}, f32[1,128,256]{2,1,0:T(8,128)S(1)}, u32[]{:S(2)}, u32[]{:S(2)}) %collective-permute-start.6) | collective-permute-done | bytes 131104 | tf_op jit(solution)/shard_map/ppermute | solution.py:19
  149.6 1.3 fusion.27
  151.0 0.2 fusion.47
  151.2 0.2 fusion.50
  151.4 0.4 fusion.48
  151.8 1.9 collective-permute-start.7
  153.7 3.4 %collective-permute-start.8 = (f32[1,128,256]{2,1,0:T(8,128)S(1)}, f32[1,128,256]{2,1,0:T(8,128)S(1)}, u32[]{:S(2)}, u32[]{:S(2)}) collective-permute-start(f32[1,128,256]{2,1,0:T(8,128)S(1)} %get-tuple-element.27), channel_id=1, source_target_pairs={{0,8},{8,16},{16,24},{24,32},{32,40},{40,48},{48,56},{56,64},{64,7... | collective-permute-start | bytes 393224 | tf_op jit(solution)/shard_map/ppermute | solution.py:19
  157.1 0.4 collective-permute-done.7
  157.5 5.2 %collective-permute-done.8 = f32[1,128,256]{2,1,0:T(8,128)S(1)} collective-permute-done((f32[1,128,256]{2,1,0:T(8,128)S(1)}, f32[1,128,256]{2,1,0:T(8,128)S(1)}, u32[]{:S(2)}, u32[]{:S(2)}) %collective-permute-start.8) | collective-permute-done | bytes 131104 | tf_op jit(solution)/shard_map/ppermute | solution.py:19
  162.7 1.3 fusion.19
  164.1 0.0 copy-start.1
  164.1 0.2 fusion.42
  164.3 0.2 fusion.45
  164.5 0.4 fusion.43
  164.9 1.9 collective-permute-start.9
  166.8 3.4 %collective-permute-start.10 = (f32[1,128,256]{2,1,0:T(8,128)S(1)}, f32[1,128,256]{2,1,0:T(8,128)S(1)}, u32[]{:S(2)}, u32[]{:S(2)}) collective-permute-start(f32[1,128,256]{2,1,0:T(8,128)S(1)} %get-tuple-element.17), channel_id=1, source_target_pairs={{0,8},{8,16},{16,24},{24,32},{32,40},{40,48},{48,56},{56,64},{64,7... | collective-permute-start | bytes 393224 | tf_op jit(solution)/shard_map/ppermute | solution.py:19
  170.2 0.4 collective-permute-done.9
  170.6 5.2 %collective-permute-done.10 = f32[1,128,256]{2,1,0:T(8,128)S(1)} collective-permute-done((f32[1,128,256]{2,1,0:T(8,128)S(1)}, f32[1,128,256]{2,1,0:T(8,128)S(1)}, u32[]{:S(2)}, u32[]{:S(2)}) %collective-permute-start.10) | collective-permute-done | bytes 131104 | tf_op jit(solution)/shard_map/ppermute | solution.py:19
  175.9 0.0 copy-done.1
  175.9 2.4 fusion.4
  178.3 0.0 all-reduce.2.cloned.1.call-update
  178.3 55.2 %all-reduce.2.cloned.1.call-done = f32[8,128,256]{2,1,0:T(8,128)} async-done(((f32[8,128,256]{2,1,0:T(8,128)}), f32[8,128,256]{2,1,0:T(8,128)}) %all-reduce.2.cloned.1.call-update) | async-done | bytes 1048592 | tf_op jit(solution)/shard_map/psum | solution.py:100
  233.6 2.4 add_bitcast_fusion
  (11 shorter events, 0.2 us)
Async XLA Ops:
  7.2 20.5 %copy-start = (f32[1,1,8,128,256]{4,3,2,1,0:T(8,128)S(1)}, f32[1,1,8,128,256]{4,3,2,1,0:T(8,128)}, u32[]{:S(2)}) copy-start(f32[1,1,8,128,256]{4,3,2,1,0:T(8,128)} %param.6) | copy-start | bytes 3145732
  8.3 19.6 %collective-permute-start = (f32[1,128,256]{2,1,0:T(8,128)S(1)}, f32[1,128,256]{2,1,0:T(8,128)S(1)}, u32[]{:S(2)}, u32[]{:S(2)}) collective-permute-start(f32[1,128,256]{2,1,0:T(8,128)S(1)} %get-tuple-element.48), channel_id=1, source_target_pairs={{8,0},{16,8},{24,16},{32,24},{40,32},{48,40},{56,48},{64,56},{72,6... | collective-permute-start | bytes 393224 | tf_op jit(solution)/shard_map/ppermute | solution.py:22
  22.4 9.0 %collective-permute-start.1 = (f32[1,128,256]{2,1,0:T(8,128)S(1)}, f32[1,128,256]{2,1,0:T(8,128)S(1)}, u32[]{:S(2)}, u32[]{:S(2)}) collective-permute-start(f32[1,128,256]{2,1,0:T(8,128)S(1)} %get-tuple-element.49), channel_id=1, source_target_pairs={{0,8},{8,16},{16,24},{24,32},{32,40},{40,48},{48,56},{56,64},{64,7... | collective-permute-start | bytes 393224 | tf_op jit(solution)/shard_map/ppermute | solution.py:19
  35.8 55.8 %copy-start.3 = (f32[4]{0:T(128)S(1)}, f32[4]{0:T(128)}, u32[]{:S(2)}) copy-start(f32[4]{0:T(128)} %constant.30.clone) | copy-start | bytes 52
  35.8 55.8 %all-to-all-start = ((f32[4,1,8,128,256]{4,3,2,1,0:T(8,128)}), f32[4,1,8,128,256]{4,3,2,1,0:T(8,128)}, u32[]{:S(2)}, u32[]{:S(2)}) async-start(f32[4,1,8,128,256]{4,3,2,1,0:T(8,128)} %stack.3), calls=%async_computation | async-start | bytes 8388608 | tf_op jit(solution)/shard_map/all_to_all | solution.py:84
  42.8 52.8 %copy-start.2 = (f32[1,8,128,256]{3,2,1,0:T(8,128)S(1)}, f32[1,8,128,256]{3,2,1,0:T(8,128)}, u32[]{:S(2)}) copy-start(f32[1,8,128,256]{3,2,1,0:T(8,128)} %param.5) | copy-start | bytes 3145732
  42.8 190.7 %all-reduce.2.cloned.1.call-start = ((), (), s32[]{:S(2)}) async-start(), calls=%async_computation.1 | async-start | bytes 2097152 | tf_op jit(solution)/shard_map/psum | solution.py:100
  43.6 57.1 %copy-start.4 = (f32[4]{0:T(128)S(1)}, f32[4]{0:T(128)}, u32[]{:S(2)}) copy-start(f32[4]{0:T(128)} %constant.29.clone) | copy-start | bytes 52
  96.8 25.0 %collective-permute-start.2 = (f32[8,128,256]{2,1,0:T(8,128)}, f32[8,128,256]{2,1,0:T(8,128)S(1)}, u32[]{:S(2)}, u32[]{:S(2)}) collective-permute-start(f32[8,128,256]{2,1,0:T(8,128)} %bitcast_add_fusion), channel_id=1, source_target_pairs={{0,1},{2,3},{4,5},{6,7},{8,9},{10,11},{12,13},{14,15},{16,17},{18,... | collective-permute-start | bytes 3145736 | tf_op jit(solution)/shard_map/ppermute | solution.py:30
  125.2 5.7 %collective-permute-start.3 = (f32[1,128,256]{2,1,0:T(8,128)S(1)}, f32[1,128,256]{2,1,0:T(8,128)S(1)}, u32[]{:S(2)}, u32[]{:S(2)}) collective-permute-start(f32[1,128,256]{2,1,0:T(8,128)S(1)} %get-tuple-element.46), channel_id=1, source_target_pairs={{8,0},{16,8},{24,16},{32,24},{40,32},{48,40},{56,48},{64,56},{72,6... | collective-permute-start | bytes 393224 | tf_op jit(solution)/shard_map/ppermute | solution.py:22
  127.5 9.0 %collective-permute-start.4 = (f32[1,128,256]{2,1,0:T(8,128)S(1)}, f32[1,128,256]{2,1,0:T(8,128)S(1)}, u32[]{:S(2)}, u32[]{:S(2)}) collective-permute-start(f32[1,128,256]{2,1,0:T(8,128)S(1)} %get-tuple-element.47), channel_id=1, source_target_pairs={{0,8},{8,16},{16,24},{24,32},{32,40},{40,48},{48,56},{56,64},{64,7... | collective-permute-start | bytes 393224 | tf_op jit(solution)/shard_map/ppermute | solution.py:19
  138.7 5.7 %collective-permute-start.5 = (f32[1,128,256]{2,1,0:T(8,128)S(1)}, f32[1,128,256]{2,1,0:T(8,128)S(1)}, u32[]{:S(2)}, u32[]{:S(2)}) collective-permute-start(f32[1,128,256]{2,1,0:T(8,128)S(1)} %get-tuple-element.36), channel_id=1, source_target_pairs={{8,0},{16,8},{24,16},{32,24},{40,32},{48,40},{56,48},{64,56},{72,6... | collective-permute-start | bytes 393224 | tf_op jit(solution)/shard_map/ppermute | solution.py:22
  140.6 9.0 %collective-permute-start.6 = (f32[1,128,256]{2,1,0:T(8,128)S(1)}, f32[1,128,256]{2,1,0:T(8,128)S(1)}, u32[]{:S(2)}, u32[]{:S(2)}) collective-permute-start(f32[1,128,256]{2,1,0:T(8,128)S(1)} %get-tuple-element.37), channel_id=1, source_target_pairs={{0,8},{8,16},{16,24},{24,32},{32,40},{40,48},{48,56},{56,64},{64,7... | collective-permute-start | bytes 393224 | tf_op jit(solution)/shard_map/ppermute | solution.py:19
  151.8 5.7 %collective-permute-start.7 = (f32[1,128,256]{2,1,0:T(8,128)S(1)}, f32[1,128,256]{2,1,0:T(8,128)S(1)}, u32[]{:S(2)}, u32[]{:S(2)}) collective-permute-start(f32[1,128,256]{2,1,0:T(8,128)S(1)} %get-tuple-element.26), channel_id=1, source_target_pairs={{8,0},{16,8},{24,16},{32,24},{40,32},{48,40},{56,48},{64,56},{72,6... | collective-permute-start | bytes 393224 | tf_op jit(solution)/shard_map/ppermute | solution.py:22
  153.7 9.0 %collective-permute-start.8 = (f32[1,128,256]{2,1,0:T(8,128)S(1)}, f32[1,128,256]{2,1,0:T(8,128)S(1)}, u32[]{:S(2)}, u32[]{:S(2)}) collective-permute-start(f32[1,128,256]{2,1,0:T(8,128)S(1)} %get-tuple-element.27), channel_id=1, source_target_pairs={{0,8},{8,16},{16,24},{24,32},{32,40},{40,48},{48,56},{56,64},{64,7... | collective-permute-start | bytes 393224 | tf_op jit(solution)/shard_map/ppermute | solution.py:19
  164.1 11.8 %copy-start.1 = (f32[8,128,256]{2,1,0:T(8,128)}, f32[8,128,256]{2,1,0:T(8,128)S(1)}, u32[]{:S(2)}) copy-start(f32[8,128,256]{2,1,0:T(8,128)S(1)} %fusion.19) | copy-start | bytes 3145732
  164.9 5.7 %collective-permute-start.9 = (f32[1,128,256]{2,1,0:T(8,128)S(1)}, f32[1,128,256]{2,1,0:T(8,128)S(1)}, u32[]{:S(2)}, u32[]{:S(2)}) collective-permute-start(f32[1,128,256]{2,1,0:T(8,128)S(1)} %get-tuple-element.16), channel_id=1, source_target_pairs={{8,0},{16,8},{24,16},{32,24},{40,32},{48,40},{56,48},{64,56},{72,6... | collective-permute-start | bytes 393224 | tf_op jit(solution)/shard_map/ppermute | solution.py:22
  166.8 9.0 %collective-permute-start.10 = (f32[1,128,256]{2,1,0:T(8,128)S(1)}, f32[1,128,256]{2,1,0:T(8,128)S(1)}, u32[]{:S(2)}, u32[]{:S(2)}) collective-permute-start(f32[1,128,256]{2,1,0:T(8,128)S(1)} %get-tuple-element.17), channel_id=1, source_target_pairs={{0,8},{8,16},{16,24},{24,32},{32,40},{40,48},{48,56},{56,64},{64,7... | collective-permute-start | bytes 393224 | tf_op jit(solution)/shard_map/ppermute | solution.py:19
Sparse Core Ops, SparseCore 0:
  178.4 55.0 all-reduce.1
